TPU v7x, 32 devices: a whole 2x2x4 slice. The times are simulated.
32 devices in a mesh: dp: 4 (over y, x), space: 8 (over z, core).
Axes of the slice: x: 2, y: 2, z: 4, core: 2. Of those that a mesh axis runs over, the one named last changes fastest.
Arguments:
- volumes: bfloat16 [4, 4, 64, 32, 512], P('dp', None, 'space'), may hold values from -6 to 6
- first_kernel: bfloat16 [3, 3, 3, 4, 32], replicated, may hold values from -0.625 to 0.625
- second_kernel: float32 [3, 3, 3, 32, 64], replicated, may hold values from -0.21875 to 0.21875
- cotangent: bfloat16 [4, 64, 16, 8, 128], P('dp', None, 'space'), may hold values from -0.5 to 0.5
- first_moment: float32 [55296], P(('dp', 'space')), may hold values from -0.75 to 0.75
- second_moment: float32 [55296], P(('dp', 'space')), may hold values from 0.001 to 0.01
Outputs:
- activations: bfloat16 [4, 64, 16, 8, 128], P('dp', None, 'space')
- first_gradient: float32 [3, 3, 3, 4, 32], replicated
- new_kernel: float32 [3, 3, 3, 32, 64], replicated
- new_first_moment: float32 [55296], P(('dp', 'space'))
- new_second_moment: float32 [55296], P(('dp', 'space'))
All inputs are finite; a program needn't handle non-finite values.
Results may differ from a plain program's by a relative error of at most 0.0055.
The roundings to bfloat16 on the way count: a program that leaves them out, or rounds other values in their place, can miss the bound.
Values may be sent and summed in bfloat16 or wider, within the bound.
No kernel may reach another device: no remote copies, remote signals or barrier semaphores. Data moves between devices by JAX's collectives and lax.ppermute only.
A program may use at most 256 MiB of HBM per device.

v0:
```python
import jax
import jax.numpy as jnp
from jax import lax
from jax.sharding import PartitionSpec as P

SLOPE = 0.3
BETA_FIRST = 0.9
BETA_SECOND = 0.999
LEARN_RATE = 0.001
EPSILON = 1e-08
NUMBERS = ("NCDHW", "DHWIO", "NCDHW")


def from_behind(value, axis, steps):
    count = lax.axis_size(axis)
    first, last = (max(0, -steps), min(count, count - steps))
    return lax.ppermute(value, axis, [(source, source + steps) for source in range(first, last)])


def strided(inputs, kernel):
    return lax.conv_general_dilated(
        inputs,
        kernel,
        (2, 2, 2),
        [(0, 0), (1, 1), (1, 1)],
        dimension_numbers=NUMBERS,
        preferred_element_type=jnp.float32,
    )


def strided_exact(inputs, kernel, depth_pad):
    return lax.conv_general_dilated(
        inputs,
        kernel,
        (2, 2, 2),
        [depth_pad, (1, 1), (1, 1)],
        dimension_numbers=NUMBERS,
        preferred_element_type=jnp.float32,
    )


def leaky(values):
    return jnp.where(values > 0, values, SLOPE * values)


def leaky_slope(values):
    return jnp.where(values > 0, jnp.float32(1.0), jnp.float32(SLOPE))


def shards(volumes, first_kernel, second_kernel, cotangent, first_moment, second_moment):
    lower_plane = from_behind(volumes[:, :, -1:], "space", 1)
    padded_in = jnp.concatenate([lower_plane, volumes], axis=2)
    preact_one = strided(padded_in, first_kernel)
    hidden = leaky(preact_one).astype(jnp.bfloat16)
    lower_hidden = from_behind(hidden[:, :, -1:], "space", 1)
    padded_hidden = jnp.concatenate([lower_hidden, hidden], axis=2)
    kernel_half = second_kernel.astype(jnp.bfloat16)
    preact_two = strided(padded_hidden, kernel_half)
    activations = leaky(preact_two).astype(jnp.bfloat16)
    delta_two = (cotangent.astype(jnp.float32) * leaky_slope(preact_two)).astype(jnp.bfloat16)
    second_wide = kernel_half.astype(jnp.float32)
    hidden_wide = padded_hidden.astype(jnp.float32)
    delta_wide = delta_two.astype(jnp.float32)

    def second_map(activ, kernel):
        return strided_exact(activ, kernel, (0, 0))

    _, pull_second = jax.vjp(second_map, hidden_wide, second_wide)
    grad_padded, second_gradient = pull_second(delta_wide)
    returned = from_behind(grad_padded[:, :, :1], "space", -1)
    grad_hidden = jnp.concatenate(
        [grad_padded[:, :, 1:-1], grad_padded[:, :, -1:] + returned], axis=2
    )
    delta_one = (grad_hidden * leaky_slope(preact_one)).astype(jnp.bfloat16)
    inputs_wide = padded_in.astype(jnp.float32)

    def first_map(kernel):
        return strided_exact(inputs_wide, kernel, (0, 0))

    _, pull_first = jax.vjp(first_map, first_kernel.astype(jnp.float32))
    (first_local,) = pull_first(delta_one.astype(jnp.float32))
    flat_grad = second_gradient.reshape(-1)
    share = first_moment.shape[0]
    offset = lax.axis_index(("dp", "space")) * share
    total_second, first_gradient = lax.psum((flat_grad, first_local), ("dp", "space"))
    grad_share = lax.dynamic_slice_in_dim(total_second, offset, share, 0)
    new_first = BETA_FIRST * first_moment + (1.0 - BETA_FIRST) * grad_share
    new_second = BETA_SECOND * second_moment + (1.0 - BETA_SECOND) * grad_share * grad_share
    kernel_share = lax.dynamic_slice_in_dim(second_kernel.reshape(-1), offset, share, 0)
    updated_share = kernel_share - LEARN_RATE * new_first / (jnp.sqrt(new_second) + EPSILON)
    new_kernel = lax.all_gather(updated_share, ("dp", "space"), axis=0, tiled=True).reshape(
        second_kernel.shape
    )
    return (activations, first_gradient, new_kernel, new_first, new_second)


def solution(mesh):
    in_specs = (
        P("dp", None, "space", None, None),
        P(),
        P(),
        P("dp", None, "space", None, None),
        P(("dp", "space")),
        P(("dp", "space")),
    )
    out_specs = (
        P("dp", None, "space", None, None),
        P(),
        P(),
        P(("dp", "space")),
        P(("dp", "space")),
    )
    return jax.shard_map(shards, mesh=mesh, in_specs=in_specs, out_specs=out_specs, check_vma=False)
```

profile of v0, /device:TPU:0, one launch (start us, length us, event | category | flops | bytes accessed | tf_op | source)
XLA Modules:
  0.0 863.5 jit_solution(15912801684704176963)
XLA Ops:
  8.2 2.4 collective-permute-start
  10.5 1.8 reshape.19
  12.4 2.1 copy.76
  14.5 1.3 constant_dynamic-update-slice_fusion
  15.8 1.1 copy-done.3
  16.9 1.9 pad
  18.8 3.9 reshape.24
  22.7 19.7 %copy.66 = bf16[4,9,32,1,8,66]{4,0,5,2,1,3:T(4,128)(2,1)} copy(bf16[4,9,32,1,8,66]{5,4,2,1,0,3:T(8,128)(2,1)S(1)} %reshape.24) | data formatting | bytes 2433024 | tf_op jit(solution)/shard_map/conv_general_dilated | solution.py:21
  42.4 1.5 slice.35
  43.9 63.5 %compare_select_fusion = (f32[4,16,8,33,32]{4,2,3,1,0:T(8,128)}, bf16[4,16,8,33,32]{4,2,3,1,0:T(8,128)(2,1)S(1)}) fusion(pred[8,33]{0,1:T(8,128)(4,1)S(1)} %copy-done.12, bf16[3,3,3,4,32]{4,3,2,1,0:T(4,128)(2,1)S(1)} %copy-done, bf16[4,9,32,1,7,2]{4,0,5,2,1,3:T(4,128)(2,1)S(1)} %slice.35, bf16[4,9,32,1,8,66]{4,0,5,2,1,3:T(4,128)(2,1)} %copy.66), kind=kOutput, calls=%fused_computation.8 | convolution fusion | flops 121356288 | bytes 4499976 | tf_op jit(solution)/shard_map/conv_general_dilated | solution.py:21
  107.6 3.9 copy.90
  111.5 1.4 copy.67
  113.8 4.6 collective-permute-start.1
  118.4 24.8 %reshape.72 = bf16[4,16,1,264,32]{4,2,3,1,0:T(2,128)(2,1)} reshape(bf16[4,16,8,33,32]{4,3,2,1,0:T(8,128)(2,1)} %copy.90) | data formatting | bytes 2162688 | tf_op jit(solution)/shard_map/convert_element_type | solution.py:54
  143.2 11.1 %slice_bitcast_fusion = bf16[1,32,4,16,256]{1,0,4,3,2:T(2,128)(2,1)} fusion(bf16[4,16,1,264,32]{4,2,3,1,0:T(2,128)(2,1)} %reshape.72), kind=kLoop, calls=%fused_computation.12 | loop fusion | bytes 2097152 | tf_op jit(solution)/shard_map/convert_element_type | solution.py:54
  154.4 80.1 %copy.86 = bf16[1,4,9,32,512]{1,0,4,3,2:T(2,128)(2,1)} copy(bf16[1,4,9,32,512]{4,3,2,1,0:T(8,128)(2,1)S(1)} %copy-done.4) | data formatting | bytes 2359296 | tf_op jit(solution)/shard_map/concatenate | solution.py:52
  234.4 10.7 %copy.85 = f32[4,16,8,33,32]{3,2,4,1,0:T(8,128)} copy(f32[4,16,8,33,32]{4,2,3,1,0:T(8,128)} %get-tuple-element.25) | data formatting | bytes 4325376 | tf_op jit(solution)/shard_map/jit(_where)/select_n | solution.py:47
  245.2 7.4 reshape.52
  252.6 1.2 copy.71
  253.8 32.8 %pad_maximum_fusion = bf16[1,32,5,16,256]{1,0,4,3,2:T(2,128)(2,1)} fusion(bf16[1,32,4,16,256]{1,0,4,3,2:T(2,128)(2,1)} %slice_bitcast_fusion, bf16[1,32,1,16,256]{1,0,4,3,2:T(2,128)(2,1)S(1)} %copy.71), kind=kLoop, calls=%fused_computation.9 | loop fusion | flops 655360 | bytes 2621440 | tf_op jit(solution)/shard_map/concatenate | solution.py:56
  286.6 13.3 %copy.72 = bf16[1,32,5,16,256]{4,3,2,1,0:T(8,128)(2,1)S(1)} copy(bf16[1,32,5,16,256]{1,0,4,3,2:T(2,128)(2,1)} %pad_maximum_fusion) | data formatting | bytes 2621440 | tf_op jit(solution)/shard_map/concatenate | solution.py:56
  300.7 5.6 reshape.31
  306.3 10.2 %copy.74 = bf16[32,5,16,1,8,34]{0,4,5,2,1,3:T(8,128)(2,1)} copy(bf16[32,5,16,1,8,34]{5,4,2,1,0,3:T(8,128)(2,1)} %reshape.31) | data formatting | bytes 2785280 | tf_op jit(solution)/shard_map/conv_general_dilated | solution.py:21
  316.4 1.2 slice.39
  317.7 7.2 compare_select_fusion.1
  325.3 25.5 %fusion.22 = f32[3,3,3,32,64]{4,3,2,1,0:T(8,128)S(1)} fusion(bf16[1,32,5,16,256]{1,0,4,3,2:T(2,128)(2,1)S(1)} %bitcast.86, bf16[1,64,2,8,128]{1,3,4,2,0:T(8,128)(2,1)S(1)} %fusion.21), kind=kOutput, calls=%fused_computation.31 | convolution fusion | flops 216489984 | bytes 1794048 | tf_op jit(solution)/shard_map/transpose(jvp())/conv_general_dilated | solution.py:32
  351.0 5.3 broadcast_select_fusion
  356.4 1.7 fusion.45
  358.1 3.4 slice.43
  362.3 8.3 copy.80
  370.6 5.9 reshape.50
  376.5 3.3 copy.83
  379.9 2.1 reshape.42
  382.8 1.3 collective-permute-start.2
  384.1 2.8 slice_bitcast_fusion.2
  386.9 1.1 copy.75
  388.1 97.6 %all-reduce.4.cloned.1.call-done = f32[55296]{0:T(1024)} async-done(((f32[55296]{0:T(1024)}), f32[55296]{0:T(1024)}) %all-reduce.4.cloned.1.call-update) | async-done | bytes 221200 | tf_op jit(solution)/shard_map/psum | solution.py:85
  485.7 1.5 subtract_dynamic-update-slice_fusion
  487.9 1.1 copy.89
  489.1 2.4 copy.81
  491.5 3.0 reshape.48
  494.5 121.3 %all-reduce.6.cloned.1.call-done = f32[55296]{0:T(1024)} async-done(((f32[55296]{0:T(1024)}), f32[55296]{0:T(1024)}) %all-reduce.6.cloned.1.call-update) | async-done | bytes 221200
  615.8 1.8 reshape.21
  617.6 1.3 fusion.30
  618.9 2.8 fusion.14
  621.7 18.4 %copy.87 = bf16[1,32,4,16,256]{1,0,4,3,2:T(2,128)(2,1)} copy(bf16[1,32,4,16,256]{4,1,3,2,0:T(8,128)(2,1)} %fusion.14) | data formatting | bytes 2097152 | tf_op jit(solution)/shard_map/convert_element_type | solution.py:74
  640.1 173.7 %fusion.46 = f32[3,3,3,4,32]{4,3,2,1,0:T(4,128)S(1)} fusion(bf16[1,4,9,32,512]{1,0,4,3,2:T(2,128)(2,1)} %copy.86, bf16[1,32,4,16,256]{1,0,4,3,2:T(2,128)(2,1)} %copy.87), kind=kOutput, calls=%fused_computation.62 | convolution fusion | flops 110742528 | bytes 2242048 | tf_op jit(solution)/shard_map/transpose(jvp())/conv_general_dilated | solution.py:32
  813.9 42.3 %psum.14 = f32[3,3,3,4,32]{4,3,2,1,0:T(4,128)} all-reduce(f32[3,3,3,4,32]{4,3,2,1,0:T(4,128)S(1)} %fusion.46), channel_id=1, replica_groups=mesh['dp'=4,'space'=8] {'dp','space'}, use_global_device_ids=true, to_apply=%region_0.1 | all-reduce | flops 3456 | bytes 27648 | tf_op jit(solution)/shard_map/psum | solution.py:85
  (57 shorter events, 5.8 us)
Async XLA Ops:
  7.2 36.8 %copy-start = (bf16[3,3,3,4,32]{4,3,2,1,0:T(4,128)(2,1)S(1)}, bf16[3,3,3,4,32]{4,3,2,1,0:T(4,128)(2,1)}, u32[]{:S(2)}) copy-start(bf16[3,3,3,4,32]{4,3,2,1,0:T(4,128)(2,1)} %param.7) | copy-start | bytes 20740
  7.2 478.5 %all-reduce.4.cloned.1.call-start = ((), (), s32[]{:S(2)}) async-start(), calls=%async_computation | async-start | bytes 442368 | tf_op jit(solution)/shard_map/psum | solution.py:85
  8.2 6.3 collective-permute-start
  15.8 1.1 copy-start.3
  22.7 21.2 %copy-start.12 = (pred[8,33]{0,1:T(8,128)(4,1)S(1)}, pred[8,33]{0,1:T(8,128)(4,1)}, u32[]{:S(2)}) copy-start(pred[8,33]{0,1:T(8,128)(4,1)} %constant.50) | copy-start | bytes 796
  113.8 138.8 %collective-permute-start.1 = (bf16[1,32,1,16,256]{4,3,2,1,0:T(8,128)(2,1)S(1)}, bf16[1,32,1,16,256]{4,3,2,1,0:T(8,128)(2,1)S(1)}, u32[]{:S(2)}, u32[]{:S(2)}) collective-permute-start(bf16[1,32,1,16,256]{4,3,2,1,0:T(8,128)(2,1)S(1)} %copy.68), channel_id=1, source_target_pairs={{0,1},{1,2},{2,3},{3,4},{4,5},{5,6},{6,7},{8,9},{9,10},{10,11},{11... | collective-permute-start | bytes 786440 | tf_op jit(solution)/shard_map/ppermute | solution.py:17
  143.2 11.1 %copy-start.4 = (bf16[1,4,9,32,512]{4,3,2,1,0:T(8,128)(2,1)S(1)}, bf16[1,4,9,32,512]{4,3,2,1,0:T(8,128)(2,1)}, u32[]{:S(2)}) copy-start(bf16[1,4,9,32,512]{4,3,2,1,0:T(8,128)(2,1)} %copy-done.3) | copy-start | bytes 3538948
  306.3 11.4 %copy-start.7 = (f32[3,3,3,32,64]{4,3,2,1,0:T(8,128)S(1)}, f32[3,3,3,32,64]{4,3,2,1,0:T(8,128)}, u32[]{:S(2)}) copy-start(f32[3,3,3,32,64]{4,3,2,1,0:T(8,128)} %param.8) | copy-start | bytes 663556
  306.3 11.4 %copy-start.13 = (pred[8,17]{0,1:T(8,128)(4,1)S(1)}, pred[8,17]{0,1:T(8,128)(4,1)}, u32[]{:S(2)}) copy-start(pred[8,17]{0,1:T(8,128)(4,1)} %constant.49) | copy-start | bytes 412
  316.4 8.8 %slice-start = ((s8[10485760]{0:T(1024)(128)(4,1)}), s8[4194304]{0:T(1024)(128)(4,1)S(1)}, s32[]{:S(2)}) async-start(s8[10485760]{0:T(1024)(128)(4,1)} %bitcast.85), calls=%async_computation.2 | async-start | bytes 8388608
  317.7 7.5 copy-start.5
  317.7 7.6 slice-start.1
  317.7 7.6 slice-start.2
  325.3 25.7 %copy-start.8 = (f32[3,3,3,32,64]{4,3,2,1,0:T(8,128)S(1)}, f32[3,3,3,32,64]{4,3,2,1,0:T(8,128)}, u32[]{:S(2)}) copy-start(f32[3,3,3,32,64]{4,3,2,1,0:T(8,128)} %param.8) | copy-start | bytes 663556
  325.3 25.7 %copy-start.11 = (pred[8,34]{0,1:T(8,128)(4,1)S(1)}, pred[8,34]{0,1:T(8,128)(4,1)}, u32[]{:S(2)}) copy-start(pred[8,34]{0,1:T(8,128)(4,1)} %constant.51) | copy-start | bytes 820
  362.3 253.5 %all-reduce.6.cloned.1.call-start = ((), (), s32[]{:S(2)}) async-start(), calls=%async_computation.1 | async-start | bytes 442368
  376.5 109.2 %copy-start.9 = (f32[1728]{0:T(1024)S(1)}, f32[1728]{0:T(1024)}, u32[]{:S(2)}) copy-start(f32[1728]{0:T(1024)} %param.10) | copy-start | bytes 20740
  376.5 109.2 %copy-start.10 = (f32[1728]{0:T(1024)S(1)}, f32[1728]{0:T(1024)}, u32[]{:S(2)}) copy-start(f32[1728]{0:T(1024)} %param.11) | copy-start | bytes 20740
  382.8 234.8 %collective-permute-start.2 = (f32[1,32,1,16,256]{4,1,3,2,0:T(8,128)}, f32[1,32,1,16,256]{4,1,3,2,0:T(8,128)}, u32[]{:S(2)}, u32[]{:S(2)}) collective-permute-start(f32[1,32,1,16,256]{4,1,3,2,0:T(8,128)} %slice_bitcast_fusion.4), channel_id=1, source_target_pairs={{1,0},{2,1},{3,2},{4,3},{5,4},{6,5},{7,6},{9,8},{10,9},{11,10},{12... | collective-permute-start | bytes 1572872 | tf_op jit(solution)/shard_map/ppermute | solution.py:17
  487.2 0.7 copy-start.6
  491.5 127.4 %copy-start.2 = (f32[4,16,1,264,32]{3,4,1,0,2:T(8,128)S(1)}, f32[4,16,1,264,32]{3,4,1,0,2:T(8,128)}, u32[]{:S(2)}) copy-start(f32[4,16,1,264,32]{3,4,1,0,2:T(8,128)} %reshape.52) | copy-start | bytes 6488068
  640.1 216.0 %copy-start.1 = (bf16[3,3,3,4,32]{4,3,2,1,0:T(4,128)(2,1)S(1)}, bf16[3,3,3,4,32]{4,3,2,1,0:T(4,128)(2,1)}, u32[]{:S(2)}) copy-start(bf16[3,3,3,4,32]{4,3,2,1,0:T(4,128)(2,1)} %param.7) | copy-start | bytes 20740
Sparse Core Ops, SparseCore 0:
  362.4 123.2 all-reduce.3
  491.8 123.9 all-reduce.5
where the time goes:
time: 877 us; the launch traced here: 863 us
  matrix products  275 us (31%)
  local copies, waits for them, and re-layouts  265 us (30%)
  waiting for transfers between devices  219 us (25%)
  blocking collectives  42.3 us (5%)
  other arithmetic  38.4 us (4%)
  between operations  14.9 us (2%)
    conv_general_dilated x3, matrix products, strided_exact(): lax.conv_general_dilated(inputs, kernel, (2, 2, 2), [depth_pad, (1, 1), (...  205 us
    unnamed x3, waiting for transfers between devices  121 us
    psum x1, waiting for transfers between devices, shards(): lax.psum((flat_grad, first_local), ('dp', 'space'))  97.6 us
    concatenate x3, local copies, waits for them, and re-layouts, shards(): padded_in = jnp.concatenate([lower_plane, volumes], axis=2)  83.2 us
    conv_general_dilated x2, matrix products, strided(): lax.conv_general_dilated(inputs, kernel, (2, 2, 2), [(0, 0), (1, 1), (1,...  70.8 us
    psum x1, blocking collectives, shards(): lax.psum((flat_grad, first_local), ('dp', 'space'))  42.3 us
    conv_general_dilated x6, local copies, waits for them, and re-layouts, strided(): lax.conv_general_dilated(inputs, kernel, (2, 2, 2), [(0, 0), (1, 1), (1,...  42.1 us
    convert_element_type x6, local copies, waits for them, and re-layouts, shards(): hidden = leaky(preact_one).astype(jnp.bfloat16)  42 us
  transfers between devices with their start and end apart: 5, of which 2 were waited for; matrix products, arithmetic and copies ran while one was open for 20% of the time, Pallas kernels for 0%

commit v1 on v0

--- a/solution.py
+++ b/solution.py
@@ -1,7 +1,9 @@
+import functools
 import jax
 import jax.numpy as jnp
 from jax import lax
 from jax.sharding import PartitionSpec as P
+from jax.lax import psum
 
 SLOPE = 0.3
 BETA_FIRST = 0.9
@@ -9,6 +11,13 @@
 LEARN_RATE = 0.001
 EPSILON = 1e-08
 NUMBERS = ("NCDHW", "DHWIO", "NCDHW")
+
+
+def windows_bring(vec, which_axis, group_axis):
+    return psum(psum(vec, axis_name=which_axis), axis_name=group_axis)
+
+
+_cut_rates = functools.partial(windows_bring, which_axis="space", group_axis="dp")
 
 
 def from_behind(value, axis, steps):
@@ -82,7 +91,7 @@
     flat_grad = second_gradient.reshape(-1)
     share = first_moment.shape[0]
     offset = lax.axis_index(("dp", "space")) * share
-    total_second, first_gradient = lax.psum((flat_grad, first_local), ("dp", "space"))
+    total_second, first_gradient = _cut_rates((flat_grad, first_local))
     grad_share = lax.dynamic_slice_in_dim(total_second, offset, share, 0)
     new_first = BETA_FIRST * first_moment + (1.0 - BETA_FIRST) * grad_share
     new_second = BETA_SECOND * second_moment + (1.0 - BETA_SECOND) * grad_share * grad_share

time: 877 us -> 844 us (0.962)
  waiting for transfers between devices: 219 us -> 178 us
    psum x1 -> x2, waiting for transfers between devices: 97.6 us -> 57.5 us  [windows_bring(): return psum(psum(vec, axis_name=which_axis), axis_name=group_axis)]
    psum x1 -> x2, blocking collectives: 42.3 us -> 45.7 us  [windows_bring(): return psum(psum(vec, axis_name=which_axis), axis_name=group_axis)]
    unnamed x3 -> x4, waiting for transfers between devices: 121 us -> 121 us
  transfers between devices with their start and end apart: 5 -> 6, of which waited for: 2 -> 3; matrix products, arithmetic and copies ran while one was open for 20% -> 22% of each run, Pallas kernels for 0% -> 0%
where the time goes in v1:
time: 844 us; the launch traced here: 831 us
  matrix products  275 us (33%)
  local copies, waits for them, and re-layouts  270 us (32%)
  waiting for transfers between devices  178 us (21%)
  blocking collectives  45.7 us (5%)
  other arithmetic  38.4 us (5%)
  between operations  14.7 us (2%)
  starting transfers between devices  8.62 us (1%)
    conv_general_dilated x3, matrix products, strided_exact(): lax.conv_general_dilated(inputs, kernel, (2, 2, 2), [depth_pad, (1, 1), (...  204 us
    unnamed x4, waiting for transfers between devices  121 us
    concatenate x3, local copies, waits for them, and re-layouts, shards(): padded_in = jnp.concatenate([lower_plane, volumes], axis=2)  82 us
    conv_general_dilated x2, matrix products, strided(): lax.conv_general_dilated(inputs, kernel, (2, 2, 2), [(0, 0), (1, 1), (1,...  70.8 us
    psum x2, waiting for transfers between devices, windows_bring(): return psum(psum(vec, axis_name=which_axis), axis_name=group_axis)  57.5 us
    psum x2, blocking collectives, windows_bring(): return psum(psum(vec, axis_name=which_axis), axis_name=group_axis)  45.7 us
    conv_general_dilated x6, local copies, waits for them, and re-layouts, strided(): lax.conv_general_dilated(inputs, kernel, (2, 2, 2), [(0, 0), (1, 1), (1,...  42.1 us
    convert_element_type x6, local copies, waits for them, and re-layouts, shards(): hidden = leaky(preact_one).astype(jnp.bfloat16)  42.1 us
  transfers between devices with their start and end apart: 6, of which 3 were waited for; matrix products, arithmetic and copies ran while one was open for 22% of the time, Pallas kernels for 0%

profile of v1, /device:TPU:0, one launch (start us, length us, event | category | flops | bytes accessed | tf_op | source)
XLA Modules:
  0.0 830.5 jit_solution(1730301900089737953)
XLA Ops:
  8.2 2.4 collective-permute-start
  10.5 1.8 reshape.19
  12.4 2.1 copy.76
  14.5 1.3 constant_dynamic-update-slice_fusion
  16.9 1.9 pad
  18.8 3.9 reshape.24
  22.7 19.7 %copy.66 = bf16[4,9,32,1,8,66]{4,0,5,2,1,3:T(4,128)(2,1)} copy(bf16[4,9,32,1,8,66]{5,4,2,1,0,3:T(8,128)(2,1)S(1)} %reshape.24) | data formatting | bytes 2433024 | tf_op jit(solution)/shard_map/conv_general_dilated | solution.py:30
  42.5 1.5 slice.35
  44.0 63.6 %compare_select_fusion = (f32[4,16,8,33,32]{4,2,3,1,0:T(8,128)}, bf16[4,16,8,33,32]{4,2,3,1,0:T(8,128)(2,1)S(1)}) fusion(pred[8,33]{0,1:T(8,128)(4,1)S(1)} %copy-done.14, bf16[3,3,3,4,32]{4,3,2,1,0:T(4,128)(2,1)S(1)} %copy-done, bf16[4,9,32,1,7,2]{4,0,5,2,1,3:T(4,128)(2,1)S(1)} %slice.35, bf16[4,9,32,1,8,66]{4,0,5,2,1,3:T(4,128)(2,1)} %copy.66), kind=kOutput, calls=%fused_computation.8 | convolution fusion | flops 121356288 | bytes 4499976 | tf_op jit(solution)/shard_map/conv_general_dilated | solution.py:30
  107.7 3.9 copy.90
  111.6 1.4 copy.67
  113.9 4.6 collective-permute-start.1
  118.5 24.8 %reshape.72 = bf16[4,16,1,264,32]{4,2,3,1,0:T(2,128)(2,1)} reshape(bf16[4,16,8,33,32]{4,3,2,1,0:T(8,128)(2,1)} %copy.90) | data formatting | bytes 2162688 | tf_op jit(solution)/shard_map/convert_element_type | solution.py:63
  143.3 11.1 %slice_bitcast_fusion = bf16[1,32,4,16,256]{1,0,4,3,2:T(2,128)(2,1)} fusion(bf16[4,16,1,264,32]{4,2,3,1,0:T(2,128)(2,1)} %reshape.72), kind=kLoop, calls=%fused_computation.12 | loop fusion | bytes 2097152 | tf_op jit(solution)/shard_map/convert_element_type | solution.py:63
  154.5 78.9 %copy.86 = bf16[1,4,9,32,512]{1,0,4,3,2:T(2,128)(2,1)} copy(bf16[1,4,9,32,512]{4,3,2,1,0:T(8,128)(2,1)S(1)} %copy-done.5) | data formatting | bytes 2359296 | tf_op jit(solution)/shard_map/concatenate | solution.py:61
  233.3 10.7 %copy.85 = f32[4,16,8,33,32]{3,2,4,1,0:T(8,128)} copy(f32[4,16,8,33,32]{4,2,3,1,0:T(8,128)} %get-tuple-element.25) | data formatting | bytes 4325376 | tf_op jit(solution)/shard_map/jit(_where)/select_n | solution.py:56
  244.0 7.4 reshape.52
  251.5 1.2 copy.71
  252.7 32.8 %pad_maximum_fusion = bf16[1,32,5,16,256]{1,0,4,3,2:T(2,128)(2,1)} fusion(bf16[1,32,4,16,256]{1,0,4,3,2:T(2,128)(2,1)} %slice_bitcast_fusion, bf16[1,32,1,16,256]{1,0,4,3,2:T(2,128)(2,1)S(1)} %copy.71), kind=kLoop, calls=%fused_computation.9 | loop fusion | flops 655360 | bytes 2621440 | tf_op jit(solution)/shard_map/concatenate | solution.py:65
  285.5 13.3 %copy.72 = bf16[1,32,5,16,256]{4,3,2,1,0:T(8,128)(2,1)S(1)} copy(bf16[1,32,5,16,256]{1,0,4,3,2:T(2,128)(2,1)} %pad_maximum_fusion) | data formatting | bytes 2621440 | tf_op jit(solution)/shard_map/concatenate | solution.py:65
  299.6 5.6 reshape.31
  305.2 10.1 %copy.74 = bf16[32,5,16,1,8,34]{0,4,5,2,1,3:T(8,128)(2,1)} copy(bf16[32,5,16,1,8,34]{5,4,2,1,0,3:T(8,128)(2,1)} %reshape.31) | data formatting | bytes 2785280 | tf_op jit(solution)/shard_map/conv_general_dilated | solution.py:30
  315.3 1.2 slice.39
  316.6 7.2 compare_select_fusion.1
  324.2 25.2 %fusion.22 = f32[3,3,3,32,64]{4,3,2,1,0:T(8,128)S(1)} fusion(bf16[1,32,5,16,256]{1,0,4,3,2:T(2,128)(2,1)S(1)} %bitcast.86, bf16[1,64,2,8,128]{1,3,4,2,0:T(8,128)(2,1)S(1)} %fusion.21), kind=kOutput, calls=%fused_computation.31 | convolution fusion | flops 216489984 | bytes 1794048 | tf_op jit(solution)/shard_map/transpose(jvp())/conv_general_dilated | solution.py:41
  350.8 5.5 broadcast_select_fusion
  356.3 4.2 copy-done.2
  360.5 1.7 fusion.45
  362.2 3.3 copy.83
  365.4 2.1 reshape.42
  368.4 6.1 slice.43
  374.5 8.3 copy.80
  382.9 6.0 reshape.50
  388.8 1.3 collective-permute-start.2
  390.1 13.0 %all-reduce.5.cloned.1.call-done = f32[55296]{0:T(1024)} async-done(((f32[55296]{0:T(1024)}), f32[55296]{0:T(1024)}) %all-reduce.5.cloned.1.call-update) | async-done | bytes 221200 | tf_op jit(solution)/shard_map/psum | solution.py:17
  403.2 2.7 slice_bitcast_fusion.2
  406.0 44.5 %all-reduce.7.cloned.1.call-done = f32[55296]{0:T(1024)} async-done(((f32[55296]{0:T(1024)}), f32[55296]{0:T(1024)}) %all-reduce.7.cloned.1.call-update) | async-done | bytes 221200 | tf_op jit(solution)/shard_map/psum | solution.py:17
  450.6 1.5 subtract_dynamic-update-slice_fusion
  453.9 2.2 copy.81
  456.1 3.0 reshape.48
  459.1 120.7 %all-reduce.9.cloned.1.call-done = f32[55296]{0:T(1024)} async-done(((f32[55296]{0:T(1024)}), f32[55296]{0:T(1024)}) %all-reduce.9.cloned.1.call-update) | async-done | bytes 221200
  579.7 1.8 reshape.21
  581.6 1.3 fusion.30
  582.9 2.7 fusion.14
  585.6 18.4 %copy.87 = bf16[1,32,4,16,256]{1,0,4,3,2:T(2,128)(2,1)} copy(bf16[1,32,4,16,256]{4,1,3,2,0:T(8,128)(2,1)} %fusion.14) | data formatting | bytes 2097152 | tf_op jit(solution)/shard_map/convert_element_type | solution.py:83
  604.0 173.7 %fusion.46 = f32[3,3,3,4,32]{4,3,2,1,0:T(4,128)S(1)} fusion(bf16[1,4,9,32,512]{1,0,4,3,2:T(2,128)(2,1)} %copy.86, bf16[1,32,4,16,256]{1,0,4,3,2:T(2,128)(2,1)} %copy.87), kind=kOutput, calls=%fused_computation.62 | convolution fusion | flops 110742528 | bytes 2242048 | tf_op jit(solution)/shard_map/transpose(jvp())/conv_general_dilated | solution.py:41
  777.7 28.3 %psum.28 = f32[3,3,3,4,32]{4,3,2,1,0:T(4,128)S(1)} all-reduce(f32[3,3,3,4,32]{4,3,2,1,0:T(4,128)S(1)} %fusion.46), channel_id=1, replica_groups=mesh['dp'=4,'space'=8] {'space'}, use_global_device_ids=true, to_apply=%region_0.1 | all-reduce | flops 3456 | bytes 27648 | tf_op jit(solution)/shard_map/psum | solution.py:17
  806.0 17.5 %psum.29 = f32[3,3,3,4,32]{4,3,2,1,0:T(4,128)} all-reduce(f32[3,3,3,4,32]{4,3,2,1,0:T(4,128)S(1)} %psum.28), channel_id=1, replica_groups=mesh['dp'=4,'space'=8] {'dp'}, use_global_device_ids=true, to_apply=%region_1.2 | all-reduce | flops 3456 | bytes 27648 | tf_op jit(solution)/shard_map/psum | solution.py:17
  (65 shorter events, 8.4 us)
Async XLA Ops:
  7.2 36.8 %copy-start = (bf16[3,3,3,4,32]{4,3,2,1,0:T(4,128)(2,1)S(1)}, bf16[3,3,3,4,32]{4,3,2,1,0:T(4,128)(2,1)}, u32[]{:S(2)}) copy-start(bf16[3,3,3,4,32]{4,3,2,1,0:T(4,128)(2,1)} %param.7) | copy-start | bytes 20740
  7.2 395.9 %all-reduce.5.cloned.1.call-start = ((), (), s32[]{:S(2)}) async-start(), calls=%async_computation | async-start | bytes 442368 | tf_op jit(solution)/shard_map/psum | solution.py:17
  8.2 6.4 collective-permute-start
  15.8 1.1 copy-start.4
  22.7 21.3 %copy-start.14 = (pred[8,33]{0,1:T(8,128)(4,1)S(1)}, pred[8,33]{0,1:T(8,128)(4,1)}, u32[]{:S(2)}) copy-start(pred[8,33]{0,1:T(8,128)(4,1)} %constant.50) | copy-start | bytes 796
  113.9 137.6 %collective-permute-start.1 = (bf16[1,32,1,16,256]{4,3,2,1,0:T(8,128)(2,1)S(1)}, bf16[1,32,1,16,256]{4,3,2,1,0:T(8,128)(2,1)S(1)}, u32[]{:S(2)}, u32[]{:S(2)}) collective-permute-start(bf16[1,32,1,16,256]{4,3,2,1,0:T(8,128)(2,1)S(1)} %copy.68), channel_id=1, source_target_pairs={{0,1},{1,2},{2,3},{3,4},{4,5},{5,6},{6,7},{8,9},{9,10},{10,11},{11... | collective-permute-start | bytes 786440 | tf_op jit(solution)/shard_map/ppermute | solution.py:26
  143.3 11.1 %copy-start.5 = (bf16[1,4,9,32,512]{4,3,2,1,0:T(8,128)(2,1)S(1)}, bf16[1,4,9,32,512]{4,3,2,1,0:T(8,128)(2,1)}, u32[]{:S(2)}) copy-start(bf16[1,4,9,32,512]{4,3,2,1,0:T(8,128)(2,1)} %copy-done.4) | copy-start | bytes 3538948
  305.2 11.4 %copy-start.9 = (f32[3,3,3,32,64]{4,3,2,1,0:T(8,128)S(1)}, f32[3,3,3,32,64]{4,3,2,1,0:T(8,128)}, u32[]{:S(2)}) copy-start(f32[3,3,3,32,64]{4,3,2,1,0:T(8,128)} %param.8) | copy-start | bytes 663556
  305.2 11.4 %copy-start.15 = (pred[8,17]{0,1:T(8,128)(4,1)S(1)}, pred[8,17]{0,1:T(8,128)(4,1)}, u32[]{:S(2)}) copy-start(pred[8,17]{0,1:T(8,128)(4,1)} %constant.49) | copy-start | bytes 412
  315.3 8.8 %slice-start = ((s8[10485760]{0:T(1024)(128)(4,1)}), s8[4194304]{0:T(1024)(128)(4,1)S(1)}, s32[]{:S(2)}) async-start(s8[10485760]{0:T(1024)(128)(4,1)} %bitcast.85), calls=%async_computation.3 | async-start | bytes 8388608
  316.5 7.4 copy-start.6
  316.6 7.5 slice-start.1
  316.6 7.5 slice-start.2
  324.1 26.6 %copy-start.10 = (f32[3,3,3,32,64]{4,3,2,1,0:T(8,128)S(1)}, f32[3,3,3,32,64]{4,3,2,1,0:T(8,128)}, u32[]{:S(2)}) copy-start(f32[3,3,3,32,64]{4,3,2,1,0:T(8,128)} %param.8) | copy-start | bytes 663556
  324.1 26.6 %copy-start.13 = (pred[8,34]{0,1:T(8,128)(4,1)S(1)}, pred[8,34]{0,1:T(8,128)(4,1)}, u32[]{:S(2)}) copy-start(pred[8,34]{0,1:T(8,128)(4,1)} %constant.51) | copy-start | bytes 820
  350.2 100.3 %all-reduce.7.cloned.1.call-start = ((), (), s32[]{:S(2)}) async-start(), calls=%async_computation.1 | async-start | bytes 442368 | tf_op jit(solution)/shard_map/psum | solution.py:17
  356.3 4.2 copy-start.2
  382.8 23.1 %copy-start.8 = (bf16[2,8,8,17,64]{4,2,3,1,0:T(8,128)(2,1)S(1)}, bf16[2,8,8,17,64]{4,2,3,1,0:T(8,128)(2,1)}, u32[]{:S(2)}) copy-start(bf16[2,8,8,17,64]{4,2,3,1,0:T(8,128)(2,1)} %get-tuple-element.28) | copy-start | bytes 835588
  382.8 67.7 %copy-start.11 = (f32[1728]{0:T(1024)S(1)}, f32[1728]{0:T(1024)}, u32[]{:S(2)}) copy-start(f32[1728]{0:T(1024)} %param.10) | copy-start | bytes 20740
  382.9 67.7 %copy-start.12 = (f32[1728]{0:T(1024)S(1)}, f32[1728]{0:T(1024)}, u32[]{:S(2)}) copy-start(f32[1728]{0:T(1024)} %param.11) | copy-start | bytes 20740
  388.8 192.7 %collective-permute-start.2 = (f32[1,32,1,16,256]{4,1,3,2,0:T(8,128)}, f32[1,32,1,16,256]{4,1,3,2,0:T(8,128)}, u32[]{:S(2)}, u32[]{:S(2)}) collective-permute-start(f32[1,32,1,16,256]{4,1,3,2,0:T(8,128)} %slice_bitcast_fusion.4), channel_id=1, source_target_pairs={{1,0},{2,1},{3,2},{4,3},{5,4},{6,5},{7,6},{9,8},{10,9},{11,10},{12... | collective-permute-start | bytes 1572872 | tf_op jit(solution)/shard_map/ppermute | solution.py:26
  403.1 176.6 %all-reduce.9.cloned.1.call-start = ((), (), s32[]{:S(2)}) async-start(), calls=%async_computation.2 | async-start | bytes 442368
  452.0 0.7 copy-start.7
  456.1 126.7 %copy-start.3 = (f32[4,16,1,264,32]{3,4,1,0,2:T(8,128)S(1)}, f32[4,16,1,264,32]{3,4,1,0,2:T(8,128)}, u32[]{:S(2)}) copy-start(f32[4,16,1,264,32]{3,4,1,0,2:T(8,128)} %reshape.52) | copy-start | bytes 6488068
  604.0 219.5 %copy-start.1 = (bf16[3,3,3,4,32]{4,3,2,1,0:T(4,128)(2,1)S(1)}, bf16[3,3,3,4,32]{4,3,2,1,0:T(4,128)(2,1)}, u32[]{:S(2)}) copy-start(bf16[3,3,3,4,32]{4,3,2,1,0:T(4,128)(2,1)} %param.7) | copy-start | bytes 20740
Sparse Core Ops, SparseCore 0:
  350.3 52.7 all-reduce.4
  406.3 44.1 all-reduce.6
  456.7 123.0 all-reduce.8
